TPU v7x, 32 devices: a whole 2x2x4 slice. The times are simulated.
32 devices in a mesh: frag: 8 (over z, x), band: 4 (over y, core).
Axes of the slice: x: 2, y: 2, z: 4, core: 2. Of those that a mesh axis runs over, the one named last changes fastest.
Arguments:
- wave_init: bfloat16 [8, 4, 64, 64, 128], P('frag', 'band'), may hold values from -6 to 6
- potential: float32 [256, 128, 128], P('frag', 'band'), may hold values from -4 to 4
- fragment_order: int32 [8, 1], P('frag'), may hold values from 0 to 15, as said below
Outputs:
- density: float32 [256, 128, 128], P('frag', 'band')
Inputs may be any that keep to these rules, and one draw needn't show every extreme that they name: `fragment_order`: every group holds at least one code q with (q % 4) // 2 == 1; a group may hold the same code in two slots.
All inputs are finite; a program needn't handle non-finite values.
Results may differ from a plain program's by a relative error of at most 0.0003.
Values sent between devices are 32-bit elements; how exact they have to be, the bound alone decides.
A program may use at most 64 MiB of HBM per device.

v0:
```python
import jax
import jax.numpy as jnp
from jax import lax
from jax.sharding import PartitionSpec as P

STEP_LENGTH = 0.1
EPSILON = 1e-06


def from_behind(block, axis, distance):
    devices = range(lax.axis_size(axis))
    route = [((i - distance) % len(devices), i) for i in devices]
    return lax.ppermute(block, axis, route)


def kinetic(extent, live_length):
    positions = jnp.arange(live_length, dtype=jnp.int32)
    angles = (positions[:, None] * positions[None, :] % live_length).astype(jnp.float32) * (
        2.0 * jnp.pi / live_length
    )
    folded = jnp.minimum(positions, live_length - positions).astype(jnp.float32)
    weight = (2.0 * jnp.pi * folded / live_length) ** 2
    cosine = jnp.cos(angles)
    sine = jnp.sin(angles)
    matrix = jnp.dot(cosine * weight[None, :], cosine.T, precision=lax.Precision.HIGHEST)
    matrix = matrix + jnp.dot(sine * weight[None, :], sine.T, precision=lax.Precision.HIGHEST)
    matrix = matrix / live_length
    return jnp.pad(matrix, ((0, extent - live_length), (0, extent - live_length)))


def geometry(slot_ids, columns, box_depth, box_width, length):
    piece_column = slot_ids // 4
    z_double = slot_ids % 4 // 2
    y_double = slot_ids % 2
    column_ids = jnp.arange(columns, dtype=jnp.int32)
    lower_pick = (piece_column[:, None] == column_ids[None, :]).astype(jnp.float32)
    upper_pick = (((piece_column + 1) % columns)[:, None] == column_ids[None, :]).astype(
        jnp.float32
    )
    z_lines = jnp.arange(box_depth, dtype=jnp.int32)
    y_lines = jnp.arange(box_width, dtype=jnp.int32)
    live_z = z_lines[None, :] < (box_depth // 2 * (1 + z_double))[:, None]
    live_y = y_lines[None, :] < (box_width // 2 * (1 + y_double))[:, None]
    live_mask = (live_z[:, :, None] & live_y[:, None, :]).astype(jnp.float32)[..., None]
    box_cells = (
        box_depth // 2 * (1 + z_double) * (box_width // 2) * (1 + y_double) * length
    ).astype(jnp.float32)
    fragment_sign = jnp.where(z_double == y_double, 1.0, -1.0).astype(jnp.float32)
    z_ops = jnp.where(
        (z_double == 1)[:, None, None],
        kinetic(box_depth, box_depth)[None],
        kinetic(box_depth, box_depth // 2)[None],
    )
    y_ops = jnp.where(
        (y_double == 1)[:, None, None],
        kinetic(box_width, box_width)[None],
        kinetic(box_width, box_width // 2)[None],
    )
    return (lower_pick, upper_pick, live_mask, box_cells, fragment_sign, z_ops, y_ops)


def hamiltonian(states, box_potential, live_mask, x_op, z_ops, y_ops):
    spectral = jnp.einsum("sbzyx,xw->sbzyw", states, x_op, precision=lax.Precision.HIGHEST)
    spectral = spectral + jnp.einsum(
        "sbzyx,szw->sbwyx", states, z_ops, precision=lax.Precision.HIGHEST
    )
    spectral = spectral + jnp.einsum(
        "sbzyx,syw->sbzwx", states, y_ops, precision=lax.Precision.HIGHEST
    )
    applied = 0.5 * spectral + box_potential[:, None] * states
    return applied * live_mask[:, None]


def gradient_step(states, box_potential, live_mask, box_cells, x_op, z_ops, y_ops):
    applied = hamiltonian(states, box_potential, live_mask, x_op, z_ops, y_ops)
    intersection = jnp.sum(states * states, axis=(2, 3, 4)) + EPSILON
    rayleigh = jnp.sum(states * applied, axis=(2, 3, 4)) / intersection
    stepped = states - STEP_LENGTH * (applied - rayleigh[:, :, None, None, None] * states)
    weight = jnp.sum(stepped * stepped, axis=(2, 3, 4)) + EPSILON
    return stepped * jnp.sqrt(box_cells[:, None] / weight)[:, :, None, None, None]


def from_region(region, lower_pick, upper_pick, columns, piece_width, length):
    region_cols = region.reshape(region.shape[0], columns, piece_width, length)
    lower_box = jnp.einsum(
        "sp,zpqx->szqx", lower_pick, region_cols, precision=lax.Precision.HIGHEST
    )
    upper_box = jnp.einsum(
        "sp,zpqx->szqx", upper_pick, region_cols, precision=lax.Precision.HIGHEST
    )
    return jnp.concatenate([lower_box, upper_box], axis=2)


def body(wave_init, potential, fragment_order):
    slot_count, band_local, box_depth, box_width, length = wave_init.shape
    slab_depth = box_depth // 2
    piece_width = box_width // 2
    columns = lax.axis_size("band")
    grid_width = piece_width * columns
    total_bands = band_local * columns
    slot_ids = fragment_order[0]
    lower_pick, upper_pick, live_mask, box_cells, fragment_sign, z_ops, y_ops = geometry(
        slot_ids, columns, box_depth, box_width, length
    )
    x_op = kinetic(length, length)
    following = from_behind(potential, "frag", -1)
    region = lax.all_gather(
        jnp.concatenate([potential, following], axis=0), "band", axis=1, tiled=True
    )
    box_potential = from_region(region, lower_pick, upper_pick, columns, piece_width, length)
    states = wave_init.astype(jnp.float32) * live_mask[:, None]
    for repeat in range(2):
        states = gradient_step(states, box_potential, live_mask, box_cells, x_op, z_ops, y_ops)
    box_density = (
        fragment_sign[:, None, None, None] * jnp.sum(states * states, axis=1) / total_bands
    )
    placed = jnp.einsum(
        "sp,szqx->zpqx",
        lower_pick,
        box_density[:, :, :piece_width],
        precision=lax.Precision.HIGHEST,
    )
    placed = placed + jnp.einsum(
        "sp,szqx->zpqx",
        upper_pick,
        box_density[:, :, piece_width:],
        precision=lax.Precision.HIGHEST,
    )
    placed = placed.reshape(2 * slab_depth, grid_width, length)
    arrived = from_behind(placed[slab_depth:], "frag", 1)
    density = lax.psum_scatter(
        placed[:slab_depth] + arrived, "band", scatter_dimension=1, tiled=True
    )
    return density


def solution(mesh):
    placed = (P("frag", "band", None, None, None), P("frag", "band", None), P("frag", None))
    return jax.shard_map(
        body, mesh=mesh, in_specs=placed, out_specs=P("frag", "band", None), check_vma=False
    )
```

profile of v0, /device:TPU:0, one launch (start us, length us, event | category | flops | bytes accessed | tf_op | source)
XLA Modules:
  0.0 196.2 jit_solution(1657264499582414949)
XLA Ops:
  6.5 6.0 %collective-permute-start = (f32[32,32,128]{2,1,0:T(8,128)}, f32[32,32,128]{2,1,0:T(8,128)S(1)}, u32[]{:S(2)}, u32[]{:S(2)}) collective-permute-start(f32[32,32,128]{2,1,0:T(8,128)} %param.4), channel_id=1, source_target_pairs={{4,0},{8,4},{12,8},{16,12},{20,16},{24,20},{28,24},{0,28},{5,1},{9... | collective-permute-start | bytes 1572872 | tf_op jit(solution)/shard_map/ppermute | solution.py:13
  12.5 11.5 %collective-permute-done = f32[32,32,128]{2,1,0:T(8,128)S(1)} collective-permute-done((f32[32,32,128]{2,1,0:T(8,128)}, f32[32,32,128]{2,1,0:T(8,128)S(1)}, u32[]{:S(2)}, u32[]{:S(2)}) %collective-permute-start) | collective-permute-done | bytes 524320 | tf_op jit(solution)/shard_map/ppermute | solution.py:13
  24.0 2.1 %pad_maximum_fusion = f32[64,32,128]{2,1,0:T(8,128)} fusion(f32[32,32,128]{2,1,0:T(8,128)S(1)} %collective-permute-done, f32[32,32,128]{2,1,0:T(8,128)} %param.4), kind=kLoop, calls=%fused_computation.42 | loop fusion | flops 262144 | bytes 2097152 | tf_op jit(solution)/shard_map/concatenate | solution.py:108
  26.2 0.0 reduce-scatter.2.cloned.1.call-start
  27.1 0.5 fusion.24
  27.6 0.5 fusion.16
  28.1 0.2 fusion.52
  28.4 0.2 fusion.18
  28.6 0.3 fusion.35
  28.9 0.1 and_convert_fusion
  29.0 0.3 fusion.17
  29.3 0.6 fusion.14
  29.9 1.8 fusion.20
  31.8 4.4 %fusion.12 = f32[64,64,128]{2,0,1:T(8,128)} fusion(f32[64,64,128]{2,1,0:T(8,128)S(1)} %fusion.14, f32[64,64]{1,0:T(8,128)S(1)} %fusion.17, f32[32,32]{1,0:T(8,128)S(1)} %fusion.18, pred[]{:T(512)} %bitcast.9), kind=kOutput, calls=%fused_computation.19 | convolution fusion | flops 402657280 | bytes 4214785 | tf_op jit(solution)/shard_map/sbzyx,szw->sbwyx/dot_general | solution.py:64
  36.2 26.4 %all-gather.2.cloned.1.call-done = f32[64,128,128]{2,1,0:T(8,128)} async-done(((f32[64,32,128]{2,1,0:T(8,128)}), f32[64,128,128]{2,1,0:T(8,128)}) %all-gather.2.cloned.1.call-update) | async-done | bytes 4194320 | tf_op jit(solution)/shard_map/all_gather | solution.py:107
  62.6 8.9 %fusion = f32[1,64,32,128]{3,0,2,1:T(1,128)S(1)} fusion(f32[64,4,32,128]{3,2,1,0:T(8,128)} %bitcast.113, s32[]{:T(128)} %bitcast.23), kind=kOutput, calls=%fused_computation.1 | convolution fusion | flops 12582916 | bytes 5242884 | tf_op jit(solution)/shard_map/sp,zpqx->szqx/dot_general | solution.py:88
  71.5 5.4 %fusion.2 = f32[1,64,32,128]{3,0,2,1:T(1,128)S(1)} fusion(f32[64,4,32,128]{3,2,1,0:T(8,128)S(1)} %bitcast.114, s32[]{:T(128)} %bitcast.16), kind=kOutput, calls=%fused_computation.3 | convolution fusion | flops 12582916 | bytes 5242884 | tf_op jit(solution)/shard_map/sp,zpqx->szqx/dot_general | solution.py:85
  76.9 6.9 %multiply_reduce_fusion.4 = (f32[]{:T(128)}, f32[]{:T(128)}, f32[1,1,64,64,128]{4,3,2,1,0:T(8,128)}) fusion(bf16[1,1,64,64,128]{4,3,2,1,0:T(8,128)(2,1)S(1)} %copy-done, f32[64,64]{1,0:T(8,128)S(1)} %and_convert_fusion, f32[1,64,32,128]{3,2,1,0:T(8,128)S(1)} %bitcast.115, f32[1,64,32,128]{3,2,1,0:T(8,128)S(1)} %bitcast.117, f32[64,64]{1,0:T(8,128)S(1)} %fusion.17, ...), kind=kOutput, calls=%fused_computation.28 | convolution fusion | flops 410521600 | bytes 9474057 | tf_op jit(solution)/shard_map/sbzyx,syw->sbzwx/dot_general | solution.py:67
  85.1 2.5 %multiply_reduce_fusion.3 = (f32[]{:T(128)}, f32[1,1,64,64,128]{4,3,2,1,0:T(8,128)S(1)}) fusion(f32[1,1,64,64,128]{4,3,2,1,0:T(8,128)} %get-tuple-element.15, f32[]{:T(128)S(6)} %div.94, f32[64,64]{1,0:T(8,128)S(1)} %and_convert_fusion, bf16[1,1,64,64,128]{4,3,2,1,0:T(8,128)(2,1)S(1)} %copy-done), kind=kLoop, calls=%fused_computation.26 | loop fusion | flops 4194303 | bytes 5259272 | tf_op jit(solution)/shard_map/reduce_sum | solution.py:79
  88.4 1.8 fusion.22
  90.2 0.2 multiply_bitcast_fusion.1
  90.5 3.0 %fusion.10 = f32[64,64,128]{2,0,1:T(8,128)S(1)} fusion(f32[64,64,128]{2,1,0:T(8,128)S(1)} %multiply_bitcast_fusion.1, f32[64,64]{1,0:T(8,128)S(1)} %fusion.17, f32[32,32]{1,0:T(8,128)S(1)} %fusion.18, pred[]{:T(512)} %bitcast.9), kind=kOutput, calls=%fused_computation.16 | convolution fusion | flops 402657280 | bytes 4214785 | tf_op jit(solution)/shard_map/sbzyx,szw->sbwyx/dot_general | solution.py:64
  93.5 6.3 %multiply_reduce_fusion.1 = (f32[]{:T(128)}, f32[]{:T(128)}, f32[1,1,64,64,128]{4,3,2,1,0:T(8,128)}) fusion(f32[1,1,64,64,128]{4,3,2,1,0:T(8,128)S(1)} %get-tuple-element.10, f32[]{:T(128)} %bitcast.33, f32[64,64]{1,0:T(8,128)S(1)} %and_convert_fusion, f32[1,64,32,128]{3,2,1,0:T(8,128)S(1)} %bitcast.116, f32[1,64,32,128]{3,2,1,0:T(8,128)S(1)} %bitcast.118, ...), kind=kOutput, calls=%fused_computation.24 | convolution fusion | flops 409473024 | bytes 10522637 | tf_op jit(solution)/shard_map/sbzyx,syw->sbzwx/dot_general | solution.py:67
  101.0 2.8 %multiply_reduce_fusion = f32[]{:T(128)} fusion(f32[1,1,64,64,128]{4,3,2,1,0:T(8,128)} %get-tuple-element.16, f32[]{:T(128)S(6)} %div.96, f32[1,1,64,64,128]{4,3,2,1,0:T(8,128)S(1)} %get-tuple-element.10, f32[]{:T(128)} %bitcast.33), kind=kLoop, calls=%fused_computation.22 | loop fusion | flops 3670015 | bytes 4194316 | tf_op jit(solution)/shard_map/reduce_sum | solution.py:79
  104.4 2.2 %multiply_bitcast_fusion = f32[1,64,64,128]{3,2,1,0:T(8,128)S(1)} fusion(f32[]{:T(128)} %bitcast.41, f32[]{:T(128)} %bitcast.4, f32[1,1,64,64,128]{4,3,2,1,0:T(8,128)} %get-tuple-element.16, f32[]{:T(128)S(6)} %div.96, f32[1,1,64,64,128]{4,3,2,1,0:T(8,128)S(1)} %get-tuple-element.10, f32[]{:T(128)} %bitcast.33), kind=kLoop, calls=%fused_computation.21 | loop fusion | flops 4718592 | bytes 6291472 | tf_op jit(solution)/shard_map/div | solution.py:115
  106.6 0.2 slice_bitcast_fusion.1
  106.8 0.9 add_bitcast_fusion
  107.7 0.8 fusion.123
  108.5 1.5 collective-permute-start.1
  110.0 49.0 %collective-permute-done.1 = f32[32,128,128]{2,1,0:T(8,128)S(1)} collective-permute-done((f32[32,128,128]{2,1,0:T(8,128)S(1)}, f32[32,128,128]{2,1,0:T(8,128)S(1)}, u32[]{:S(2)}, u32[]{:S(2)}) %collective-permute-start.1) | collective-permute-done | bytes 2097184 | tf_op jit(solution)/shard_map/ppermute | solution.py:13
  159.0 1.6 bitcast_add_fusion.2
  160.7 28.6 %reduce-scatter.2.cloned.1.call-done = f32[32,32,128]{2,1,0:T(8,128)} async-done(((f32[32,128,128]{2,1,0:T(8,128)}), f32[32,32,128]{2,1,0:T(8,128)}) %reduce-scatter.2.cloned.1.call-update) | async-done | bytes 524304 | tf_op jit(solution)/shard_map/reduce_scatter | solution.py:131
  (22 shorter events, 0.1 us)
Async XLA Ops:
  6.5 56.0 %all-gather.2.cloned.1.call-start = ((), (), s32[]{:S(2)}) async-start(), calls=%async_computation.1 | async-start | bytes 5242880 | tf_op jit(solution)/shard_map/all_gather | solution.py:107
  6.5 17.5 %collective-permute-start = (f32[32,32,128]{2,1,0:T(8,128)}, f32[32,32,128]{2,1,0:T(8,128)S(1)}, u32[]{:S(2)}, u32[]{:S(2)}) collective-permute-start(f32[32,32,128]{2,1,0:T(8,128)} %param.4), channel_id=1, source_target_pairs={{4,0},{8,4},{12,8},{16,12},{20,16},{24,20},{28,24},{0,28},{5,1},{9... | collective-permute-start | bytes 1572872 | tf_op jit(solution)/shard_map/ppermute | solution.py:13
  26.1 3.2 %copy-start = (bf16[1,1,64,64,128]{4,3,2,1,0:T(8,128)(2,1)S(1)}, bf16[1,1,64,64,128]{4,3,2,1,0:T(8,128)(2,1)}, u32[]{:S(2)}) copy-start(bf16[1,1,64,64,128]{4,3,2,1,0:T(8,128)(2,1)} %param.3) | copy-start | bytes 3145732
  26.2 163.2 %reduce-scatter.2.cloned.1.call-start = ((), (), s32[]{:S(2)}) async-start(), calls=%async_computation.2 | async-start | bytes 2621440 | tf_op jit(solution)/shard_map/reduce_scatter | solution.py:131
  62.6 8.9 %copy-start.1 = (f32[64,128,128]{2,1,0:T(8,128)S(1)}, f32[64,128,128]{2,1,0:T(8,128)}, u32[]{:S(2)}) copy-start(f32[64,128,128]{2,1,0:T(8,128)} %all-gather.2.cloned.1.call-done) | copy-start | bytes 12582916
  71.5 5.4 %copy-start.2 = (f32[1,64,32,128]{3,0,2,1:T(1,128)}, f32[1,64,32,128]{3,0,2,1:T(1,128)S(1)}, u32[]{:S(2)}) copy-start(f32[1,64,32,128]{3,0,2,1:T(1,128)S(1)} %fusion) | copy-start | bytes 3145732
  71.5 5.4 %copy-start.6 = (f32[64,64,128]{2,0,1:T(8,128)S(1)}, f32[64,64,128]{2,0,1:T(8,128)}, u32[]{:S(2)}) copy-start(f32[64,64,128]{2,0,1:T(8,128)} %fusion.12) | copy-start | bytes 6291460
  76.9 6.9 %copy-start.4 = (f32[1,64,32,128]{3,0,2,1:T(1,128)}, f32[1,64,32,128]{3,0,2,1:T(1,128)S(1)}, u32[]{:S(2)}) copy-start(f32[1,64,32,128]{3,0,2,1:T(1,128)S(1)} %fusion.2) | copy-start | bytes 3145732
  90.4 3.1 %copy-start.3 = (f32[1,64,32,128]{3,0,2,1:T(1,128)S(1)}, f32[1,64,32,128]{3,0,2,1:T(1,128)}, u32[]{:S(2)}) copy-start(f32[1,64,32,128]{3,0,2,1:T(1,128)} %copy-done.2) | copy-start | bytes 3145732
  90.5 3.1 %copy-start.5 = (f32[1,64,32,128]{3,0,2,1:T(1,128)S(1)}, f32[1,64,32,128]{3,0,2,1:T(1,128)}, u32[]{:S(2)}) copy-start(f32[1,64,32,128]{3,0,2,1:T(1,128)} %copy-done.4) | copy-start | bytes 3145732
  108.5 50.5 %collective-permute-start.1 = (f32[32,128,128]{2,1,0:T(8,128)S(1)}, f32[32,128,128]{2,1,0:T(8,128)S(1)}, u32[]{:S(2)}, u32[]{:S(2)}) collective-permute-start(f32[32,128,128]{2,1,0:T(8,128)S(1)} %bitcast.119), channel_id=1, source_target_pairs={{28,0},{0,4},{4,8},{8,12},{12,16},{16,20},{20,24},{24,28},{29,1},{... | collective-permute-start | bytes 6291464 | tf_op jit(solution)/shard_map/ppermute | solution.py:13
Sparse Core Ops, SparseCore 0:
  26.3 36.2 all-gather.1
  160.8 28.4 reduce-scatter.1
where the time goes:
time: 196 us
  waiting for transfers between devices  116 us (59%)
  matrix products  40.5 us (21%)
  between operations  18.4 us (9%)
  other arithmetic  13.1 us (7%)
  starting transfers between devices  7.57 us (4%)
    ppermute x2, waiting for transfers between devices, from_behind(): return lax.ppermute(block, axis, route)  60.5 us
    reduce_scatter x1, waiting for transfers between devices, body(): lax.psum_scatter(placed[:slab_depth] + arrived, 'band', scatter_dimension...  28.6 us
    all_gather x1, waiting for transfers between devices, body(): lax.all_gather(jnp.concatenate([potential, following], axis=0), 'band', a...  26.4 us
    dot_general x2, matrix products, hamiltonian(): jnp.einsum('sbzyx,syw->sbzwx', states, y_ops, precision=lax.Precision.HIG...  13.1 us
    dot_general x1, matrix products, from_region(): jnp.einsum('sp,zpqx->szqx', upper_pick, region_cols, precision=lax.Precis...  8.87 us
    ppermute x2, starting transfers between devices, from_behind(): return lax.ppermute(block, axis, route)  7.52 us
    dot_general x2, matrix products, hamiltonian(): jnp.einsum('sbzyx,szw->sbwyx', states, z_ops, precision=lax.Precision.HIG...  7.39 us
    dot_general x1, matrix products, from_region(): jnp.einsum('sp,zpqx->szqx', lower_pick, region_cols, precision=lax.Precis...  5.4 us
  transfers between devices with their start and end apart: 4, of which 4 were waited for; matrix products, arithmetic and copies ran while one was open for 5% of the time, Pallas kernels for 0%

commit v1 on v0

v1 whole, which is shorter than its diff:
```python
import functools

import jax
import jax.numpy as jnp
import numpy as np
from jax import lax
from jax.experimental import pallas as pl
from jax.experimental.pallas import tpu as pltpu
from jax.sharding import PartitionSpec as P

STEP_LENGTH = 0.1
EPSILON = 1e-06
MESH = pl.DeviceIdType.MESH
PARTS = 4


def half_kinetic(extent, live_length):
    m = np.arange(live_length)
    weight = (2.0 * np.pi * np.minimum(m, live_length - m) / live_length) ** 2
    gap = m[:, None] - m[None, :]
    matrix = np.einsum(
        "m,mij->ij", weight, np.cos(2.0 * np.pi * (m[:, None, None] * gap[None] % live_length) / live_length)
    )
    full = np.zeros((extent, extent))
    full[:live_length, :live_length] = 0.5 * matrix / live_length
    return full


def two_parts(matrix):
    high = matrix.astype(jnp.bfloat16)
    low = (matrix - high.astype(np.float64)).astype(jnp.bfloat16)
    return high, low


def x_operator(length):
    high, low = two_parts(half_kinetic(length, length))
    return np.block([[high, low], [high, np.zeros_like(high)]]).astype(jnp.bfloat16)


def line_operators(extent):
    rows = []
    for live in (extent // 2, extent):
        high, low = two_parts(half_kinetic(extent, live))
        rows.append(np.concatenate([high, low, high], axis=1))
    return np.stack(rows).astype(jnp.bfloat16)


def fold(block):
    return jnp.sum(block.reshape(-1, 8, block.shape[-1]), axis=0)


def dot(a, b):
    return jnp.dot(a, b, preferred_element_type=jnp.float32)


def split(block):
    high = block.astype(jnp.bfloat16)
    return high, (block - high.astype(jnp.float32)).astype(jnp.bfloat16)


def kernel(
    n_frag, n_band, depth, width, length,
    code_ref, wave_ref, pot_ref, kx_ref, kz_ref, ky_ref, out_ref,
    state, applied, box, columns, picked, mine, before,
    to_pair, from_pair, upper, above, lower, to_chip, from_chip, kept, last, ending,
    code_sem, pair_sem, chip_sem, relay_sem, pick_sem, rise_sem,
    half_sem, up_sem, row_sem, end_sem,
):
    g = lax.axis_index("frag")
    b = lax.axis_index("band")
    core = lax.rem(b, 2)
    chip = lax.div(b, 2)
    chips = n_band // 2
    after_g = lax.rem(g + 1, n_frag)
    before_g = lax.rem(g + n_frag - 1, n_frag)
    pair = (g, chip * 2 + 1 - core)
    others = [lax.rem(chip + d, chips) for d in range(1, chips)]
    sources = [lax.rem(chip + chips - d, chips) for d in range(1, chips)]
    slab = depth // 2
    piece = width // 2
    sent = []

    def send(src, dst, sems, index, device):
        copy = pltpu.make_async_remote_copy(
            src_ref=src, dst_ref=dst, send_sem=sems.at[(0, *index)], recv_sem=sems.at[(1, *index)],
            device_id=device, device_id_type=MESH,
        )
        copy.start()
        sent.append(copy)
        return copy

    code = code_ref[0, 0]
    column = lax.shift_right_logical(code, 2)
    z_double = lax.bitwise_and(lax.shift_right_logical(code, 1), 1)
    y_double = lax.bitwise_and(code, 1)
    mine[...] = jnp.full(mine.shape, code, jnp.int32)

    barrier = pltpu.get_barrier_semaphore()
    peers = [pair, (after_g, b), (before_g, b)] + [(g, 2 * o + core) for o in others]
    for peer in peers:
        pl.semaphore_signal(barrier, inc=1, device_id=peer, device_id_type=MESH)
    pl.semaphore_wait(barrier, len(peers))

    step = slab // PARTS
    code_copy = send(mine, before, code_sem, (0,), (after_g, b))
    pair_copies, chip_copies = [], []
    for c in range(PARTS):
        rows = pl.ds(c * step, step)
        chip_copies.append([
            send(pot_ref.at[rows], columns.at[b, rows], chip_sem, (i, c), (g, 2 * o + core))
            for i, o in enumerate(others)
        ])
        pair_copies.append(send(pot_ref.at[rows], columns.at[b, rows], pair_sem, (c,), pair))
    columns[b] = pot_ref[...]

    y_live = lax.broadcasted_iota(jnp.int32, (width, length), 0) < piece * (1 + y_double)

    def begin(z, carry):
        rows = pl.ds(pl.multiple_of(z * width, width), width)
        live = jnp.logical_and(y_live, z < slab * (1 + z_double))
        state[rows, :] = jnp.where(live, wave_ref[rows, :].astype(jnp.float32), 0.0)
        return carry

    lax.fori_loop(0, depth, begin, 0, unroll=4)

    def along_z(first, count, exact):
        op = kz_ref[z_double]
        op = op[:, : 2 * depth] if exact else op

        def one(i, carry):
            y = first + 2 * i
            parts = []
            for e in range(2):
                block = state[pl.ds(y + e, depth, stride=width), :]
                if exact:
                    high = block.astype(jnp.bfloat16)
                    parts.append(jnp.concatenate([high, high], axis=0))
                else:
                    high, low = split(block)
                    parts.append(jnp.concatenate([high, high, low], axis=0))
            result = dot(op, jnp.concatenate(parts, axis=1))
            for e in range(2):
                applied[pl.ds(y + e, depth, stride=width), :] = result[:, e * length : (e + 1) * length]
            return carry

        lax.fori_loop(0, count // 2, one, 0, unroll=4)

    def along_xy(z, exact):
        rows = pl.ds(pl.multiple_of(z * width, 2 * width), 2 * width)
        block = state[rows, :]
        op = ky_ref[y_double]
        if exact:
            high = block.astype(jnp.bfloat16)
            wide = dot(high, kx_ref[0:length, :])
            parts = [jnp.concatenate([high[e * width : (e + 1) * width]] * 2, axis=0) for e in range(2)]
            op = op[:, : 2 * width]
        else:
            high, low = split(block)
            wide = dot(jnp.concatenate([high, low], axis=1), kx_ref[...])
            parts = []
            for e in range(2):
                own = slice(e * width, (e + 1) * width)
                parts.append(jnp.concatenate([high[own], high[own], low[own]], axis=0))
        tall = dot(op, jnp.concatenate(parts, axis=1))
        total = applied[rows, :] + (wide[:, :length] + wide[:, length:])
        total = total + jnp.concatenate([tall[:, :length], tall[:, length:]], axis=0)
        return rows, block, total

    def first_xy(first, count):
        def one(i, carry):
            rows, _, total = along_xy(first + 2 * i, True)
            applied[rows, :] = total
            return carry

        lax.fori_loop(0, count // 2, one, 0, unroll=4)

    picks, rises = [], []

    def relay_columns(c):
        rows = pl.ds(c * step, step)
        relays = []
        for i, s in enumerate(sources):
            chip_copies[c][i].wait_recv()
            here = columns.at[2 * s + core, rows]
            relays.append(send(here, here, relay_sem, (i, c), pair))
        pair_copies[c].wait_recv()
        return relays

    def pick_column(c, relays):
        rows = pl.ds(c * step, step)
        for relay in relays:
            relay.wait_recv()
        if c == 0:
            code_copy.wait_recv()
        target = lax.rem(lax.shift_right_logical(before[0:1, :], 2) + core, n_band)
        value = columns[0, rows]
        for n in range(1, n_band):
            value = jnp.where(jnp.broadcast_to((target == n)[None], value.shape), columns[n, rows], value)
        picked[c] = value
        picks.append(send(
            picked.at[c], box.at[pl.ds(slab + c * step, step), core], pick_sem, (c,), (before_g, b)
        ))

    def pass_up(c):
        picks[c].wait_recv()
        here = box.at[pl.ds(slab + c * step, step), core]
        rises.append(send(here, here, rise_sem, (c,), pair))

    half = width // 2
    along_z(0, half, True)
    relays = relay_columns(0)
    along_z(half, width - half, True)
    pick_column(0, relays)
    relays = relay_columns(1)
    first_xy(0, depth // 2)
    pick_column(1, relays)
    relays = relay_columns(2)
    pass_up(0)
    first_xy(depth // 2, depth // 2)
    pick_column(2, relays)
    relays = relay_columns(3)
    pass_up(1)
    pick_column(3, relays)

    next_column = lax.rem(column + 1, n_band)

    def lower_box(z, carry):
        box[z, 0] = columns[column, z]
        box[z, 1] = columns[next_column, z]
        return carry

    lax.fori_loop(0, slab, lower_box, 0, unroll=4)

    def first_full(first, count, sums):
        def one(i, carry):
            own, cross = carry
            z = first + i
            rows = pl.ds(pl.multiple_of(z * width, width), width)
            s = state[rows, :]
            h = applied[rows, :] + box[z].reshape(width, length) * s
            applied[rows, :] = h
            return own + fold(s * s), cross + fold(s * h)

        return lax.fori_loop(0, count, one, sums, unroll=4)

    zero = jnp.zeros((8, length), jnp.float32)
    sums = first_full(0, slab, (zero, zero))
    pass_up(2)
    pass_up(3)
    for c in range(PARTS):
        rises[c].wait_recv()
        sums = first_full(slab + c * step, step, sums)

    def whole(block):
        return jnp.sum(block, axis=(0, 1), keepdims=True)

    rayleigh = whole(sums[1]) / (whole(sums[0]) + EPSILON)
    gain = 1.0 + STEP_LENGTH * rayleigh

    def advance(z, carry):
        rows = pl.ds(pl.multiple_of(z * width, width), width)
        t = gain * state[rows, :] - STEP_LENGTH * applied[rows, :]
        state[rows, :] = t
        return carry + fold(t * t)

    weight = whole(lax.fori_loop(0, depth, advance, zero, unroll=4))

    along_z(0, width, False)

    def second(i, carry):
        cross, square = carry
        z = 2 * i
        rows, t, total = along_xy(z, False)
        h = total + box[pl.ds(z, 2)].reshape(2 * width, length) * t
        applied[rows, :] = h
        return cross + fold(t * h), square + fold(h * h)

    cross, square = lax.fori_loop(0, depth // 2, second, (zero, zero), unroll=2)
    cross, square = whole(cross), whole(square)

    cells = (slab * piece * length * (1 + z_double) * (1 + y_double)).astype(jnp.float32)
    scale1 = cells / (weight + EPSILON)
    rayleigh = scale1 * cross / (scale1 * weight + EPSILON)
    gain = 1.0 + STEP_LENGTH * rayleigh
    stepped = gain * gain * weight - 2.0 * STEP_LENGTH * gain * cross + STEP_LENGTH * STEP_LENGTH * square
    scale2 = cells / (scale1 * stepped + EPSILON)
    sign = jnp.where(z_double == y_double, 1.0, -1.0).astype(jnp.float32) / n_band
    factor = sign * scale1 * scale2

    share = slab // 2
    lines = share // PARTS

    def density(z):
        rows = pl.ds(pl.multiple_of(z * width, width), lines * width)
        u = gain * state[rows, :] - STEP_LENGTH * applied[rows, :]
        return (factor * (u * u)).reshape(lines, 2, piece, length)

    halves = {}
    def give(level, j):
        to_pair[level, j] = density(level * slab + share * (1 - core) + lines * j)
        halves[level, j] = send(to_pair.at[level, j], from_pair.at[level, j], half_sem, (level, j), pair)

    def take(level, j):
        own = density(level * slab + share * core + lines * j)
        halves[level, j].wait_recv()
        return own + from_pair[level, j]

    ups = []
    give(1, 0)
    for j in range(PARTS):
        if j + 1 < PARTS:
            give(1, j + 1)
        upper[j] = take(1, j)
        ups.append(send(upper.at[j], above.at[j], up_sem, (j,), (after_g, b)))
    for j in range(PARTS):
        give(0, j)
    for j in range(PARTS):
        lower[j] = take(0, j)

    before_column = lax.shift_right_logical(before[0:1, :], 2)
    before_next = lax.rem(before_column + 1, n_band)

    def onto(n, j):
        shape = (lines, piece, length)
        value = jnp.where(column == n, lower[j, :, 0], 0.0) + jnp.where(next_column == n, lower[j, :, 1], 0.0)
        left = jnp.broadcast_to((before_column == n)[None], shape)
        right = jnp.broadcast_to((before_next == n)[None], shape)
        return value + jnp.where(left, above[j, :, 0], 0.0) + jnp.where(right, above[j, :, 1], 0.0)

    crossings = []

    def place(j):
        ups[j].wait_recv()
        row = []
        for i, o in enumerate(others):
            for e in range(2):
                to_chip[i, j, e] = onto(2 * o + e, j)
            row.append(send(to_chip.at[i, j], from_chip.at[i, j], row_sem, (i, j), (g, 2 * o + core)))
        crossings.append(row)
        for e in range(2):
            kept[j, e] = onto(2 * chip + e, j)

    endings = []

    def finish(j):
        own, given = kept[j, core], kept[j, 1 - core]
        for i, copy in enumerate(crossings[j]):
            copy.wait_recv()
            own = own + from_chip[i, j, core]
            given = given + from_chip[i, j, 1 - core]
        last[j] = given
        endings.append(send(last.at[j], ending.at[j], end_sem, (j,), pair))
        out_ref[pl.ds(share * core + lines * j, lines)] = own

    for j in range(PARTS):
        place(j)
        if j > 0:
            finish(j - 1)
    finish(PARTS - 1)
    for j in range(PARTS):
        endings[j].wait_recv()
        out_ref[pl.ds(share * (1 - core) + lines * j, lines)] = ending[j]
    for copy in sent:
        copy.wait_send()


def body(n_frag, n_band, wave_init, potential, fragment_order):
    slots, bands, depth, width, length = wave_init.shape
    assert slots == 1 and bands == 1 and n_band % 2 == 0
    slab, piece = potential.shape[:2]
    others = n_band // 2 - 1
    share = slab // 2
    lines = share // PARTS
    f32 = jnp.float32
    dma = pltpu.SemaphoreType.DMA
    part = (PARTS, lines, 2, piece, length)
    chip_part = (others, PARTS, 2, lines, piece, length)
    vmem = pl.BlockSpec(memory_space=pltpu.VMEM)
    return pl.pallas_call(
        functools.partial(kernel, n_frag, n_band, depth, width, length),
        out_shape=jax.ShapeDtypeStruct((slab, piece, length), f32),
        in_specs=[pl.BlockSpec(memory_space=pltpu.SMEM)] + [vmem] * 5,
        out_specs=vmem,
        scratch_shapes=[
            pltpu.VMEM((depth * width, length), f32),
            pltpu.VMEM((depth * width, length), f32),
            pltpu.VMEM((depth, 2, piece, length), f32),
            pltpu.VMEM((n_band, slab, piece, length), f32),
            pltpu.VMEM((PARTS, slab // PARTS, piece, length), f32),
            pltpu.VMEM((8, 128), jnp.int32),
            pltpu.VMEM((8, 128), jnp.int32),
            pltpu.VMEM((2, *part), f32),
            pltpu.VMEM((2, *part), f32),
            pltpu.VMEM(part, f32),
            pltpu.VMEM(part, f32),
            pltpu.VMEM(part, f32),
            pltpu.VMEM(chip_part, f32),
            pltpu.VMEM(chip_part, f32),
            pltpu.VMEM((PARTS, 2, lines, piece, length), f32),
            pltpu.VMEM((PARTS, lines, piece, length), f32),
            pltpu.VMEM((PARTS, lines, piece, length), f32),
            dma((2, 1)),
            dma((2, PARTS)),
            dma((2, others, PARTS)),
            dma((2, others, PARTS)),
            dma((2, PARTS)),
            dma((2, PARTS)),
            dma((2, 2, PARTS)),
            dma((2, PARTS)),
            dma((2, others, PARTS)),
            dma((2, PARTS)),
        ],
        compiler_params=pltpu.CompilerParams(
            collective_id=0, has_side_effects=True, vmem_limit_bytes=60 * 1024 * 1024
        ),
        name="fragment_step",
    )(
        fragment_order,
        wave_init.reshape(depth * width, length),
        potential,
        jnp.asarray(x_operator(length)),
        jnp.asarray(line_operators(depth)),
        jnp.asarray(line_operators(width)),
    )


def solution(mesh):
    placed = (P("frag", "band", None, None, None), P("frag", "band", None), P("frag", None))
    return jax.shard_map(
        functools.partial(body, mesh.shape["frag"], mesh.shape["band"]),
        mesh=mesh, in_specs=placed, out_specs=P("frag", "band", None), check_vma=False,
    )
```

time: 196 us -> 62.7 us (0.32)
  waiting for transfers between devices: 116 us -> 0 us
  Pallas kernels: 0 us -> 59.9 us
  matrix products: 40.5 us -> 0 us
  between operations: 18.4 us -> 0.66 us
  other arithmetic: 13.1 us -> 0 us
  starting transfers between devices: 7.57 us -> 0 us
    ppermute x2 -> x0, waiting for transfers between devices: 60.5 us -> none  [from_behind(): return lax.ppermute(block, axis, route)]
    pallas_call x0 -> x1, Pallas kernels: none -> 59.9 us  [body(): pl.pallas_call(functools.partial(kernel, n_frag, n_band, depth, width, le...]
    dot_general x14 -> x0, matrix products: 40.5 us -> none  [the longest x2 13.1 us: hamiltonian(): jnp.einsum('sbzyx,syw->sbzwx', states, y_ops, precision=lax.Precision.HIG...]
    reduce_scatter x1 -> x0, waiting for transfers between devices: 28.6 us -> none  [body(): lax.psum_scatter(placed[:slab_depth] + arrived, 'band', scatter_dimension...]
    all_gather x1 -> x0, waiting for transfers between devices: 26.4 us -> none  [body(): lax.all_gather(jnp.concatenate([potential, following], axis=0), 'band', a...]
    ppermute x2 -> x0, starting transfers between devices: 7.52 us -> none  [from_behind(): return lax.ppermute(block, axis, route)]
    reduce_sum x2 -> x0, other arithmetic: 5.29 us -> none  [gradient_step(): weight = jnp.sum(stepped * stepped, axis=(2, 3, 4)) + EPSILON]
    add x2 -> x0, other arithmetic: 2.52 us -> none  [the longest x1 1.64 us: body(): placed[:slab_depth] + arrived]
  transfers between devices with their start and end apart: 4 -> 0, of which waited for: 4 -> 0; matrix products, arithmetic and copies ran while one was open for 5% -> 0% of each run, Pallas kernels for 0% -> 0%
where the time goes in v1:
time: 62.7 us; the launch traced here: 62.5 us
  Pallas kernels  59.9 us (96%)
  local copies, waits for them, and re-layouts  1.87 us (3%)
  between operations  0.66 us (1%)
    pallas_call x1, Pallas kernels, body(): pl.pallas_call(functools.partial(kernel, n_frag, n_band, depth, width, le...  59.9 us
    unnamed x1, local copies, waits for them, and re-layouts  1.87 us

profile of v1, /device:TPU:0, one launch (start us, length us, event | category | flops | bytes accessed | tf_op | source)
XLA Modules:
  0.0 62.5 jit_solution(4620955857883938295)
XLA Ops:
  0.7 59.9 %fragment_step.1 = f32[32,32,128]{2,1,0:T(8,128)} custom-call(s32[1,1]{1,0:T(1,128)S(6)} %copy.8.code_ref, bf16[4096,128]{1,0:T(8,128)(2,1)} %bitcast.1, f32[32,32,128]{2,1,0:T(8,128)} %pot_ref.1, bf16[256,256]{1,0:T(8,128)(2,1)} %constant.4.clone.kx_ref, bf16[2,64,192]{2,1,0:T(8,128)(2,1)} %constant.5.clone.kz_ref.ky_ref, ...), custom_call_target="tpu_custom_call" | custom-call | tf_op jit(solution)/shard_map/fragment_step/pallas_call | solution.py:379
  60.6 1.9 %copy.9 = f32[32,32,128]{2,1,0:T(8,128)} copy(f32[32,32,128]{2,1,0:T(8,128)} %fragment_step.1) | data formatting | bytes 1048576

commit v2 on v1

v2 whole, which is shorter than its diff:
```python
import functools

import jax
import jax.numpy as jnp
import numpy as np
from jax import lax
from jax.experimental import pallas as pl
from jax.experimental.pallas import tpu as pltpu
from jax.sharding import PartitionSpec as P

STEP_LENGTH = 0.1
EPSILON = 1e-06
MESH = pl.DeviceIdType.MESH
PARTS = 8
VMEM_BYTES = 40 * 1024 * 1024


def half_kinetic(extent, live_length):
    m = np.arange(live_length)
    weight = (2.0 * np.pi * np.minimum(m, live_length - m) / live_length) ** 2
    gap = m[:, None] - m[None, :]
    matrix = np.einsum(
        "m,mij->ij", weight, np.cos(2.0 * np.pi * (m[:, None, None] * gap[None] % live_length) / live_length)
    )
    full = np.zeros((extent, extent))
    full[:live_length, :live_length] = 0.5 * matrix / live_length
    return full


def two_parts(matrix):
    high = matrix.astype(jnp.bfloat16)
    low = (matrix - high.astype(np.float64)).astype(jnp.bfloat16)
    return high, low


def x_operator(length):
    high, low = two_parts(half_kinetic(length, length))
    return np.block([[high, low], [high, np.zeros_like(high)]]).astype(jnp.bfloat16)


def line_operators(extent, by_half):
    rows, halved = [], []
    for live in (extent // 2, extent):
        high, low = two_parts(half_kinetic(extent, live))
        rows.append(np.concatenate([high, low, high], axis=1))
        cut = extent // 2
        halved.append(np.concatenate(
            [part[:, own] for own in (slice(0, cut), slice(cut, extent)) for part in (high, low, high)], axis=1
        ))
    return np.stack(halved + rows if by_half else rows).astype(jnp.bfloat16)


def fold(block):
    return jnp.sum(block.reshape(-1, 8, block.shape[-1]), axis=0)


def dot(a, b):
    return jnp.dot(a, b, preferred_element_type=jnp.float32)


def split(block):
    high = block.astype(jnp.bfloat16)
    return high, (block - high.astype(jnp.float32)).astype(jnp.bfloat16)


def kernel(
    n_frag, n_band, depth, width, length,
    code_ref, wave_hbm, pot_ref, kx_hbm, kz_hbm, ky_hbm, out_ref,
    wave_ref, kx_ref, kz_ref, ky_ref, state, applied, twice, lifted, box, columns, picked, mine, before,
    to_pair, from_pair, upper, above, lower, to_chip, from_chip, kept, ending,
    load_sem, code_sem, pair_sem, chip_send, chip_recv, relay_sem, pick_sem, rise_sem,
    half_sem, up_sem, row_send, row_recv, end_sem,
):
    g = lax.axis_index("frag")
    b = lax.axis_index("band")
    core = lax.rem(b, 2)
    chip = lax.div(b, 2)
    chips = n_band // 2
    after_g = lax.rem(g + 1, n_frag)
    before_g = lax.rem(g + n_frag - 1, n_frag)
    pair = (g, chip * 2 + 1 - core)
    others = [lax.rem(chip + d, chips) for d in range(1, chips)]
    sources = [lax.rem(chip + chips - d, chips) for d in range(1, chips)]
    slab = depth // 2
    piece = width // 2
    share = slab // 2
    lines = share // PARTS
    sent = []

    def transfer(src, dst, send_sem, recv_sem, device):
        return pltpu.make_async_remote_copy(
            src_ref=src, dst_ref=dst, send_sem=send_sem, recv_sem=recv_sem,
            device_id=device, device_id_type=MESH,
        )

    def send(src, dst, sems, index, device):
        copy = transfer(src, dst, sems.at[(0, *index)], sems.at[(1, *index)], device)
        copy.start()
        sent.append(copy)
        return copy

    barrier = pltpu.get_barrier_semaphore()
    peers = [pair, (after_g, b), (before_g, b)] + [(g, 2 * o + e) for o in others for e in range(2)]
    for peer in peers:
        pl.semaphore_signal(barrier, inc=1, device_id=peer, device_id_type=MESH)
    loads = [
        pltpu.make_async_copy(src, dst, load_sem.at[n])
        for n, (src, dst) in enumerate((
            (wave_hbm, wave_ref), (kz_hbm, kz_ref), (kx_hbm, kx_ref), (ky_hbm, ky_ref), (pot_ref, columns.at[b])
        ))
    ]
    for load in loads:
        load.start()
    code = code_ref[0, 0]
    column = lax.shift_right_logical(code, 2)
    next_column = lax.rem(column + 1, n_band)
    z_double = lax.bitwise_and(lax.shift_right_logical(code, 1), 1)
    y_double = lax.bitwise_and(code, 1)
    mine[...] = jnp.full(mine.shape, code, jnp.int32)
    pl.semaphore_wait(barrier, len(peers))

    def slab_rows(half, j):
        return pl.ds(share * half + lines * j, lines)

    pair_copies = {}
    for j in range(PARTS):
        for i, o in enumerate(others):
            for e in range(2):
                rows = slab_rows(e, j)
                copy = transfer(
                    pot_ref.at[rows], columns.at[b, rows],
                    chip_send.at[i, e, j], chip_recv.at[i, core, j], (g, 2 * o + e),
                )
                copy.start()
                sent.append(copy)
        if j == 0:
            code_copy = send(mine, before, code_sem, (0,), (after_g, b))
        rows = slab_rows(1 - core, j)
        pair_copies[j] = send(pot_ref.at[rows], columns.at[b, rows], pair_sem, (0, j), pair)
    for j in range(PARTS):
        rows = slab_rows(core, j)
        pair_copies[PARTS + j] = send(pot_ref.at[rows], columns.at[b, rows], pair_sem, (1, j), pair)

    for load in loads[:2]:
        load.wait()
    y_live = lax.broadcasted_iota(jnp.int32, (width, length), 0) < piece * (1 + y_double)

    def begin(z, carry):
        rows = pl.ds(pl.multiple_of(z * width, width), width)
        live = jnp.logical_and(y_live, z < slab * (1 + z_double))
        state[rows, :] = jnp.where(live, wave_ref[rows, :].astype(jnp.float32), 0.0)
        return carry

    lax.fori_loop(0, depth, begin, 0, unroll=4)

    def first_z(first, count):
        op = kz_ref[2 + z_double][:, : 2 * depth]

        def one(i, carry):
            y = first + 2 * i
            parts = []
            for e in range(2):
                high = state[pl.ds(y + e, depth, stride=width), :].astype(jnp.bfloat16)
                parts.append(jnp.concatenate([high, high], axis=0))
            result = dot(op, jnp.concatenate(parts, axis=1))
            for e in range(2):
                applied[pl.ds(y + e, depth, stride=width), :] = result[:, e * length : (e + 1) * length]
            return carry

        lax.fori_loop(0, count // 2, one, 0, unroll=4)

    def two_rows(z):
        return pl.ds(pl.multiple_of(z * width, 2 * width), 2 * width)

    def first_xy(first, count):
        op = ky_ref[y_double][:, : 2 * width]

        def one(i, carry):
            rows = two_rows(first + 2 * i)
            high = state[rows, :].astype(jnp.bfloat16)
            wide = dot(high, kx_ref[0:length, :])
            parts = [jnp.concatenate([high[e * width : (e + 1) * width]] * 2, axis=0) for e in range(2)]
            tall = dot(op, jnp.concatenate(parts, axis=1))
            total = applied[rows, :] + (wide[:, :length] + wide[:, length:])
            applied[rows, :] = total + jnp.concatenate([tall[:, :length], tall[:, length:]], axis=0)
            return carry

        lax.fori_loop(0, count // 2, one, 0, unroll=4)

    picks, rises = [], []
    relays = []

    def pick_part(j):
        rows = slab_rows(core, j)
        pair_copies[j].wait_recv()
        for i, s in enumerate(sources):
            for e in range(2):
                here = columns.at[2 * s + e, rows]
                transfer(here, here, chip_send.at[i, e, j], chip_recv.at[i, e, j], pair).wait_recv()
        if j == 0:
            code_copy.wait_recv()
            loads[4].wait()
        base = lax.shift_right_logical(before[0:1, :], 2)
        for side in range(2):
            target = lax.rem(base + side, n_band)
            value = columns[0, rows]
            for n in range(1, n_band):
                value = jnp.where(jnp.broadcast_to((target == n)[None], value.shape), columns[n, rows], value)
            picked[j, :, side] = value
        place_at = pl.ds(slab + share * core + lines * j, lines)
        picks.append(send(picked.at[j], box.at[place_at], pick_sem, (j,), (before_g, b)))
        for i, s in enumerate(sources):
            for e in range(2):
                here = columns.at[2 * s + e, rows]
                relays.append(send(here, here, relay_sem, (i, e, j), pair))

    def pass_up(j):
        picks[j].wait_recv()
        here = box.at[pl.ds(slab + share * core + lines * j, lines)]
        rises.append(send(here, here, rise_sem, (j,), pair))

    quarter = width // 4
    first_z(0, quarter)
    first_z(quarter, quarter)
    pick_part(0)
    first_z(2 * quarter, quarter)
    first_z(3 * quarter, quarter)
    pick_part(1)
    loads[2].wait()
    loads[3].wait()
    quarter = depth // 4
    ready = 2
    for n in range(4):
        first_xy(n * quarter, quarter)
        pick_part(ready)
        ready += 1
        if n > 0:
            pass_up(n - 1)
    passed = 3
    while ready < PARTS:
        pick_part(ready)
        ready += 1
        pass_up(passed)
        passed += 1

    for j in range(PARTS):
        pair_copies[PARTS + j].wait_recv()
    for relay in relays:
        relay.wait_recv()

    def lower_box(z, carry):
        box[z, 0] = columns[column, z]
        box[z, 1] = columns[next_column, z]
        return carry

    lax.fori_loop(0, slab, lower_box, 0, unroll=4)

    def full_rows(z, sums):
        rows = two_rows(z)
        s = state[rows, :]
        v = box[pl.ds(z, 2)].reshape(2 * width, length)
        h = applied[rows, :] + v * s
        applied[rows, :] = h
        return (sums[0] + fold(s * s), sums[1] + fold(s * h), sums[2] + fold(h * h)), h, v

    def again_xy(z, h, v):
        rows = two_rows(z)
        high, low = split(h)
        wide = dot(jnp.concatenate([high, low], axis=1), kx_ref[...])
        parts = []
        for e in range(2):
            own = slice(e * width, (e + 1) * width)
            parts.append(jnp.concatenate([high[own], high[own], low[own]], axis=0))
        tall = dot(ky_ref[y_double], jnp.concatenate(parts, axis=1))
        total = v * h + (wide[:, :length] + wide[:, length:])
        twice[rows, :] = total + jnp.concatenate([tall[:, :length], tall[:, length:]], axis=0)

    def both(z, sums):
        sums, h, v = full_rows(z, sums)
        again_xy(z, h, v)
        return sums

    def z_parts(y, level):
        parts = []
        for e in range(2):
            high, low = split(applied[pl.ds(level * slab * width + y + e, slab, stride=width), :])
            parts.append(jnp.concatenate([high, high, low], axis=0))
        return jnp.concatenate(parts, axis=1)

    zero = jnp.zeros((8, length), jnp.float32)
    sums = (zero, zero, zero)
    while passed < PARTS:
        pass_up(passed)
        passed += 1
    sums = lax.fori_loop(0, slab // 2, lambda i, c: both(2 * i, c), sums, unroll=4)
    op = kz_ref[z_double]

    def low_z(i, carry):
        y = 2 * i
        result = dot(op[:, : 3 * slab], z_parts(y, 0))
        for e in range(2):
            lifted[pl.ds(y + e, depth, stride=width), :] = result[:, e * length : (e + 1) * length]
        return carry

    lax.fori_loop(0, width // 2, low_z, 0, unroll=4)
    for j in range(PARTS):
        for i in range(lines // 2):
            sums = both(slab + share * core + lines * j + 2 * i, sums)
    for j in range(PARTS):
        rises[j].wait_recv()
        for i in range(lines // 2):
            sums = both(slab + share * (1 - core) + lines * j + 2 * i, sums)

    def high_z(i, carry):
        cross, square = carry
        y = 2 * i
        result = dot(op[:, 3 * slab :], z_parts(y, 1))
        for e in range(2):
            at = pl.ds(y + e, depth, stride=width)
            total = twice[at, :] + lifted[at, :] + result[:, e * length : (e + 1) * length]
            twice[at, :] = total
            cross = cross + fold(applied[at, :] * total)
            square = square + fold(total * total)
        return cross, square

    cross, square = lax.fori_loop(0, width // 2, high_z, (zero, zero), unroll=4)

    def whole(block):
        return jnp.sum(block, axis=(0, 1), keepdims=True)

    ss, sh, hh = (whole(part) for part in sums)
    hb, bb = whole(cross), whole(square)
    tau = STEP_LENGTH
    a = 1.0 + tau * (sh / (ss + EPSILON))
    tt = a * a * ss - 2.0 * tau * a * sh + tau * tau * hh
    th = a * a * sh - 2.0 * tau * a * hh + tau * tau * hb
    qq = a * a * hh - 2.0 * tau * a * hb + tau * tau * bb
    cells = (slab * piece * length * (1 + z_double) * (1 + y_double)).astype(jnp.float32)
    scale1 = cells / (tt + EPSILON)
    a2 = 1.0 + tau * (scale1 * th / (scale1 * tt + EPSILON))
    uu = a2 * a2 * tt - 2.0 * tau * a2 * th + tau * tau * qq
    scale2 = cells / (scale1 * uu + EPSILON)
    sign = jnp.where(z_double == y_double, 1.0, -1.0).astype(jnp.float32) / n_band
    factor = sign * scale1 * scale2
    by_s, by_h, by_b = a2 * a, tau * (a2 + a), tau * tau

    def density(z):
        rows = pl.ds(pl.multiple_of(z * width, width), lines * width)
        u = by_s * state[rows, :] - by_h * applied[rows, :] + by_b * twice[rows, :]
        return (factor * (u * u)).reshape(lines, 2, piece, length)

    halves = {}

    def give(level, j):
        to_pair[level, j] = density(level * slab + share * (1 - core) + lines * j)
        halves[level, j] = send(to_pair.at[level, j], from_pair.at[level, j], half_sem, (level, j), pair)

    def take(level, j):
        own = density(level * slab + share * core + lines * j)
        halves[level, j].wait_recv()
        return own + from_pair[level, j]

    ups = []
    give(1, 0)
    give(1, 1)
    for j in range(PARTS):
        if j + 2 < PARTS:
            give(1, j + 2)
        upper[j] = take(1, j)
        ups.append(send(upper.at[j], above.at[j], up_sem, (j,), (after_g, b)))
    for j in range(PARTS):
        give(0, j)

    before_column = lax.shift_right_logical(before[0:1, :], 2)
    before_next = lax.rem(before_column + 1, n_band)

    def onto(n, j):
        shape = (lines, piece, length)
        value = jnp.where(column == n, lower[j, :, 0], 0.0) + jnp.where(next_column == n, lower[j, :, 1], 0.0)
        left = jnp.broadcast_to((before_column == n)[None], shape)
        right = jnp.broadcast_to((before_next == n)[None], shape)
        return value + jnp.where(left, above[j, :, 0], 0.0) + jnp.where(right, above[j, :, 1], 0.0)

    endings = []

    def place(j):
        lower[j] = take(0, j)
        ups[j].wait_recv()
        for i, o in enumerate(others):
            for e in range(2):
                to_chip[i, j, e] = onto(2 * o + e, j)
                copy = transfer(
                    to_chip.at[i, j, e], from_chip.at[i, core, j],
                    row_send.at[i, e, j], row_recv.at[i, core, j], (g, 2 * o + e),
                )
                copy.start()
                sent.append(copy)
        kept[0, j] = onto(2 * chip + 1 - core, j)
        endings.append(send(kept.at[0, j], ending.at[j], end_sem, (j,), pair))
        kept[1, j] = onto(b, j)

    def finish(j):
        endings[j].wait_recv()
        for half, own in ((core, kept[1, j]), (1 - core, ending[j])):
            for i in range(len(others)):
                here = from_chip.at[i, half, j]
                transfer(here, here, row_send.at[i, 0, j], row_recv.at[i, half, j], pair).wait_recv()
                own = own + from_chip[i, half, j]
            out_ref[slab_rows(half, j)] = own

    for j in range(PARTS):
        place(j)
        if j > 2:
            finish(j - 3)
    for j in range(PARTS - 3, PARTS):
        finish(j)
    for copy in sent:
        copy.wait_send()


def body(n_frag, n_band, wave_init, potential, fragment_order):
    slots, bands, depth, width, length = wave_init.shape
    assert slots == 1 and bands == 1 and n_band % 2 == 0
    slab, piece = potential.shape[:2]
    others = n_band // 2 - 1
    share = slab // 2
    lines = share // PARTS
    f32 = jnp.float32
    dma = pltpu.SemaphoreType.DMA
    part = (PARTS, lines, 2, piece, length)
    flat = (depth * width, length)
    column_part = (lines, piece, length)
    constants = (x_operator(length), line_operators(depth, True), line_operators(width, False))
    anywhere = pl.BlockSpec(memory_space=pltpu.HBM)
    return pl.pallas_call(
        functools.partial(kernel, n_frag, n_band, depth, width, length),
        out_shape=jax.ShapeDtypeStruct((slab, piece, length), f32),
        in_specs=[pl.BlockSpec(memory_space=pltpu.SMEM)] + [anywhere] * 5,
        out_specs=pl.BlockSpec(memory_space=pltpu.VMEM),
        scratch_shapes=[
            pltpu.VMEM(flat, jnp.bfloat16),
            *[pltpu.VMEM(constant.shape, jnp.bfloat16) for constant in constants],
            pltpu.VMEM(flat, f32),
            pltpu.VMEM(flat, f32),
            pltpu.VMEM(flat, f32),
            pltpu.VMEM(flat, f32),
            pltpu.VMEM((depth, 2, piece, length), f32),
            pltpu.VMEM((n_band, slab, piece, length), f32),
            pltpu.VMEM(part, f32),
            pltpu.VMEM((8, 128), jnp.int32),
            pltpu.VMEM((8, 128), jnp.int32),
            pltpu.VMEM((2, *part), f32),
            pltpu.VMEM((2, *part), f32),
            pltpu.VMEM(part, f32),
            pltpu.VMEM(part, f32),
            pltpu.VMEM(part, f32),
            pltpu.VMEM((others, PARTS, 2, *column_part), f32),
            pltpu.VMEM((others, 2, PARTS, *column_part), f32),
            pltpu.VMEM((2, PARTS, *column_part), f32),
            pltpu.VMEM((PARTS, *column_part), f32),
            dma((5,)),
            dma((2, 1)),
            dma((2, 2, PARTS)),
            dma((others, 2, PARTS)),
            dma((others, 2, PARTS)),
            dma((2, others, 2, PARTS)),
            dma((2, PARTS)),
            dma((2, PARTS)),
            dma((2, 2, PARTS)),
            dma((2, PARTS)),
            dma((others, 2, PARTS)),
            dma((others, 2, PARTS)),
            dma((2, PARTS)),
        ],
        compiler_params=pltpu.CompilerParams(
            collective_id=0, has_side_effects=True, vmem_limit_bytes=VMEM_BYTES
        ),
        name="fragment_step",
    )(
        fragment_order,
        wave_init.reshape(flat),
        potential,
        *[jnp.asarray(constant) for constant in constants],
    )


def solution(mesh):
    placed = (P("frag", "band", None, None, None), P("frag", "band", None), P("frag", None))
    return jax.shard_map(
        functools.partial(body, mesh.shape["frag"], mesh.shape["band"]),
        mesh=mesh, in_specs=placed, out_specs=P("frag", "band", None), check_vma=False,
    )
```

time: 62.7 us -> 63.4 us (1.011)
  local copies, waits for them, and re-layouts: 1.87 us -> 5.7 us
  Pallas kernels: 59.9 us -> 56.8 us
    unnamed x1 -> x11, local copies, waits for them, and re-layouts: 1.87 us -> 5.7 us
    pallas_call x1, Pallas kernels: 59.9 us -> 56.8 us  [body(): pl.pallas_call(functools.partial(kernel, n_frag, n_band, depth, width, le...]
where the time goes in v2:
time: 63.4 us; the launch traced here: 63.1 us
  Pallas kernels  56.8 us (90%)
  local copies, waits for them, and re-layouts  5.7 us (9%)
  between operations  0.67 us (1%)
    pallas_call x1, Pallas kernels, body(): pl.pallas_call(functools.partial(kernel, n_frag, n_band, depth, width, le...  56.8 us
    unnamed x11, local copies, waits for them, and re-layouts  5.7 us

profile of v2, /device:TPU:0, one launch (start us, length us, event | category | flops | bytes accessed | tf_op | source)
XLA Modules:
  0.0 63.1 jit_solution(676939004377517569)
XLA Ops:
  0.7 0.0 copy-start
  0.7 1.2 %copy-done = bf16[1,1,64,64,128]{4,3,2,1,0:T(8,128)(2,1)S(1)} copy-done((bf16[1,1,64,64,128]{4,3,2,1,0:T(8,128)(2,1)S(1)}, bf16[1,1,64,64,128]{4,3,2,1,0:T(8,128)(2,1)}, u32[]{:S(2)}) %copy-start) | copy-done | bytes 1048600
  1.9 0.0 copy-start.1
  1.9 1.0 %copy-done.1 = f32[32,32,128]{2,1,0:T(8,128)S(1)} copy-done((f32[32,32,128]{2,1,0:T(8,128)S(1)}, f32[32,32,128]{2,1,0:T(8,128)}, u32[]{:S(2)}) %copy-start.1) | copy-done | bytes 524312
  2.9 0.0 copy-start.2
  2.9 0.9 %copy-done.2 = bf16[4,64,192]{2,1,0:T(8,128)(2,1)S(1)} copy-done((bf16[4,64,192]{2,1,0:T(8,128)(2,1)S(1)}, bf16[4,64,192]{2,1,0:T(8,128)(2,1)}, u32[]{:S(2)}) %copy-start.2) | copy-done | bytes 98328
  3.8 0.0 copy-start.3
  3.8 0.9 %copy-done.3 = bf16[256,256]{1,0:T(8,128)(2,1)S(1)} copy-done((bf16[256,256]{1,0:T(8,128)(2,1)S(1)}, bf16[256,256]{1,0:T(8,128)(2,1)}, u32[]{:S(2)}) %copy-start.3) | copy-done | bytes 131096
  4.7 0.0 copy-start.4
  4.7 0.8 %copy-done.4 = bf16[2,64,192]{2,1,0:T(8,128)(2,1)S(1)} copy-done((bf16[2,64,192]{2,1,0:T(8,128)(2,1)S(1)}, bf16[2,64,192]{2,1,0:T(8,128)(2,1)}, u32[]{:S(2)}) %copy-start.4) | copy-done | bytes 49176
  5.6 56.8 %fragment_step.1 = f32[32,32,128]{2,1,0:T(8,128)S(1)} custom-call(s32[1,1]{1,0:T(1,128)S(6)} %copy.8.code_ref, bf16[4096,128]{1,0:T(8,128)(2,1)S(1)} %bitcast.1, f32[32,32,128]{2,1,0:T(8,128)S(1)} %copy-done.1, bf16[256,256]{1,0:T(8,128)(2,1)S(1)} %copy-done.3, bf16[4,64,192]{2,1,0:T(8,128)(2,1)S(1)} %copy-done.2, bf16[2,64,192]{2,1,0:T(8,128)(2,1)S(1)} %copy-done.4), custom_call_target="tpu_custom_call" | custom-call | tf_op jit(solution)/shard_map/fragment_step/pallas_call | solution.py:435
  62.3 0.8 %copy.9 = f32[32,32,128]{2,1,0:T(8,128)} copy(f32[32,32,128]{2,1,0:T(8,128)S(1)} %fragment_step.1) | data formatting | bytes 1048576
Async XLA Ops:
  0.7 1.2 %copy-start = (bf16[1,1,64,64,128]{4,3,2,1,0:T(8,128)(2,1)S(1)}, bf16[1,1,64,64,128]{4,3,2,1,0:T(8,128)(2,1)}, u32[]{:S(2)}) copy-start(bf16[1,1,64,64,128]{4,3,2,1,0:T(8,128)(2,1)} %param.6) | copy-start | bytes 3145732
  1.9 1.0 %copy-start.1 = (f32[32,32,128]{2,1,0:T(8,128)S(1)}, f32[32,32,128]{2,1,0:T(8,128)}, u32[]{:S(2)}) copy-start(f32[32,32,128]{2,1,0:T(8,128)} %pot_ref.1) | copy-start | bytes 1572868
  2.9 0.9 %copy-start.2 = (bf16[4,64,192]{2,1,0:T(8,128)(2,1)S(1)}, bf16[4,64,192]{2,1,0:T(8,128)(2,1)}, u32[]{:S(2)}) copy-start(bf16[4,64,192]{2,1,0:T(8,128)(2,1)} %constant.7.clone.kz_hbm) | copy-start | bytes 294916
  3.8 0.9 %copy-start.3 = (bf16[256,256]{1,0:T(8,128)(2,1)S(1)}, bf16[256,256]{1,0:T(8,128)(2,1)}, u32[]{:S(2)}) copy-start(bf16[256,256]{1,0:T(8,128)(2,1)} %constant.6.clone.kx_hbm) | copy-start | bytes 393220
  4.7 0.8 %copy-start.4 = (bf16[2,64,192]{2,1,0:T(8,128)(2,1)S(1)}, bf16[2,64,192]{2,1,0:T(8,128)(2,1)}, u32[]{:S(2)}) copy-start(bf16[2,64,192]{2,1,0:T(8,128)(2,1)} %constant.8.clone.ky_hbm) | copy-start | bytes 147460

commit v3 on v2

--- a/solution.py
+++ b/solution.py
@@ -12,7 +12,8 @@
 EPSILON = 1e-06
 MESH = pl.DeviceIdType.MESH
 PARTS = 8
-VMEM_BYTES = 40 * 1024 * 1024
+PAD = 8
+VMEM_BYTES = 62 * 1024 * 1024
 
 
 def half_kinetic(extent, live_length):
@@ -38,16 +39,12 @@
     return np.block([[high, low], [high, np.zeros_like(high)]]).astype(jnp.bfloat16)
 
 
-def line_operators(extent, by_half):
-    rows, halved = [], []
+def line_operators(extent):
+    rows = []
     for live in (extent // 2, extent):
         high, low = two_parts(half_kinetic(extent, live))
         rows.append(np.concatenate([high, low, high], axis=1))
-        cut = extent // 2
-        halved.append(np.concatenate(
-            [part[:, own] for own in (slice(0, cut), slice(cut, extent)) for part in (high, low, high)], axis=1
-        ))
-    return np.stack(halved + rows if by_half else rows).astype(jnp.bfloat16)
+    return np.stack(rows).astype(jnp.bfloat16)
 
 
 def fold(block):
@@ -66,7 +63,7 @@
 def kernel(
     n_frag, n_band, depth, width, length,
     code_ref, wave_hbm, pot_ref, kx_hbm, kz_hbm, ky_hbm, out_ref,
-    wave_ref, kx_ref, kz_ref, ky_ref, state, applied, twice, lifted, box, columns, picked, mine, before,
+    wave_ref, kx_ref, kz_ref, ky_ref, state, applied, twice, box, columns, picked, mine, before,
     to_pair, from_pair, upper, above, lower, to_chip, from_chip, kept, ending,
     load_sem, code_sem, pair_sem, chip_send, chip_recv, relay_sem, pick_sem, rise_sem,
     half_sem, up_sem, row_send, row_recv, end_sem,
@@ -85,6 +82,7 @@
     piece = width // 2
     share = slab // 2
     lines = share // PARTS
+    pitch = width + PAD
     sent = []
 
     def transfer(src, dst, send_sem, recv_sem, device):
@@ -148,47 +146,53 @@
     def begin(z, carry):
         rows = pl.ds(pl.multiple_of(z * width, width), width)
         live = jnp.logical_and(y_live, z < slab * (1 + z_double))
-        state[rows, :] = jnp.where(live, wave_ref[rows, :].astype(jnp.float32), 0.0)
+        state[pl.ds(pl.multiple_of(z * pitch, 8), width), :] = jnp.where(live, wave_ref[rows, :].astype(jnp.float32), 0.0)
         return carry
 
     lax.fori_loop(0, depth, begin, 0, unroll=4)
 
     def first_z(first, count):
-        op = kz_ref[2 + z_double][:, : 2 * depth]
+        op = kz_ref[z_double][:, : 2 * depth]
 
         def one(i, carry):
             y = first + 2 * i
             parts = []
             for e in range(2):
-                high = state[pl.ds(y + e, depth, stride=width), :].astype(jnp.bfloat16)
+                high = state[pl.ds(y + e, depth, stride=pitch), :].astype(jnp.bfloat16)
                 parts.append(jnp.concatenate([high, high], axis=0))
             result = dot(op, jnp.concatenate(parts, axis=1))
             for e in range(2):
-                applied[pl.ds(y + e, depth, stride=width), :] = result[:, e * length : (e + 1) * length]
+                applied[pl.ds(y + e, depth, stride=pitch), :] = result[:, e * length : (e + 1) * length]
             return carry
 
         lax.fori_loop(0, count // 2, one, 0, unroll=4)
 
-    def two_rows(z):
-        return pl.ds(pl.multiple_of(z * width, 2 * width), 2 * width)
+    def lines_of(ref, z, count=2):
+        return jnp.concatenate(
+            [ref[pl.ds(pl.multiple_of((z + n) * pitch, 8), width), :] for n in range(count)], axis=0
+        )
+
+    def put_two(ref, z, value):
+        for n in range(2):
+            ref[pl.ds(pl.multiple_of((z + n) * pitch, 8), width), :] = value[n * width : (n + 1) * width]
 
     def first_xy(first, count):
         op = ky_ref[y_double][:, : 2 * width]
 
         def one(i, carry):
-            rows = two_rows(first + 2 * i)
-            high = state[rows, :].astype(jnp.bfloat16)
+            z = first + 2 * i
+            high = lines_of(state, z).astype(jnp.bfloat16)
             wide = dot(high, kx_ref[0:length, :])
             parts = [jnp.concatenate([high[e * width : (e + 1) * width]] * 2, axis=0) for e in range(2)]
             tall = dot(op, jnp.concatenate(parts, axis=1))
-            total = applied[rows, :] + (wide[:, :length] + wide[:, length:])
-            applied[rows, :] = total + jnp.concatenate([tall[:, :length], tall[:, length:]], axis=0)
+            total = lines_of(applied, z) + (wide[:, :length] + wide[:, length:])
+            put_two(applied, z, total + jnp.concatenate([tall[:, :length], tall[:, length:]], axis=0))
             return carry
 
         lax.fori_loop(0, count // 2, one, 0, unroll=4)
 
     picks, rises = [], []
-    relays = []
+    relays = {}
 
     def pick_part(j):
         rows = slab_rows(core, j)
@@ -212,12 +216,58 @@
         for i, s in enumerate(sources):
             for e in range(2):
                 here = columns.at[2 * s + e, rows]
-                relays.append(send(here, here, relay_sem, (i, e, j), pair))
+                relays[i, e, j] = send(here, here, relay_sem, (i, e, j), pair)
 
     def pass_up(j):
         picks[j].wait_recv()
         here = box.at[pl.ds(slab + share * core + lines * j, lines)]
         rises.append(send(here, here, rise_sem, (j,), pair))
+
+    def full_rows(z, sums):
+        s = lines_of(state, z)
+        v = box[pl.ds(z, 2)].reshape(2 * width, length)
+        h = lines_of(applied, z) + v * s
+        put_two(applied, z, h)
+        return (sums[0] + fold(s * s), sums[1] + fold(s * h), sums[2] + fold(h * h)), h, v
+
+    def again_xy(z, h, v):
+        high, low = split(h)
+        wide = dot(jnp.concatenate([high, low], axis=1), kx_ref[...])
+        parts = []
+        for e in range(2):
+            own = slice(e * width, (e + 1) * width)
+            parts.append(jnp.concatenate([high[own], high[own], low[own]], axis=0))
+        tall = dot(ky_ref[y_double], jnp.concatenate(parts, axis=1))
+        total = v * h + (wide[:, :length] + wide[:, length:])
+        put_two(twice, z, total + jnp.concatenate([tall[:, :length], tall[:, length:]], axis=0))
+
+    def both(z, sums):
+        sums, h, v = full_rows(z, sums)
+        again_xy(z, h, v)
+        return sums
+
+    zero = jnp.zeros((8, length), jnp.float32)
+    sums = (zero, zero, zero)
+    def lower_part(j, sums):
+        pair_copies[PARTS + j].wait_recv()
+        for i in range(len(others)):
+            for e in range(2):
+                relays[i, e, j].wait_recv()
+        for half in range(2):
+            rows = slab_rows(half, j)
+            for side, target in enumerate((column, next_column)):
+                value = columns[0, rows]
+                for n in range(1, n_band):
+                    value = jnp.where(target == n, columns[n, rows], value)
+                box[rows, side] = value
+            for i in range(lines // 2):
+                sums = both(share * half + lines * j + 2 * i, sums)
+        return sums
+
+    def upper_part(half, j, sums):
+        for i in range(lines // 2):
+            sums = both(slab + share * half + lines * j + 2 * i, sums)
+        return sums
 
     quarter = width // 4
     first_z(0, quarter)
@@ -229,101 +279,47 @@
     loads[2].wait()
     loads[3].wait()
     quarter = depth // 4
-    ready = 2
-    for n in range(4):
-        first_xy(n * quarter, quarter)
-        pick_part(ready)
-        ready += 1
-        if n > 0:
-            pass_up(n - 1)
-    passed = 3
-    while ready < PARTS:
-        pick_part(ready)
-        ready += 1
-        pass_up(passed)
-        passed += 1
-
-    for j in range(PARTS):
-        pair_copies[PARTS + j].wait_recv()
-    for relay in relays:
-        relay.wait_recv()
-
-    def lower_box(z, carry):
-        box[z, 0] = columns[column, z]
-        box[z, 1] = columns[next_column, z]
-        return carry
-
-    lax.fori_loop(0, slab, lower_box, 0, unroll=4)
-
-    def full_rows(z, sums):
-        rows = two_rows(z)
-        s = state[rows, :]
-        v = box[pl.ds(z, 2)].reshape(2 * width, length)
-        h = applied[rows, :] + v * s
-        applied[rows, :] = h
-        return (sums[0] + fold(s * s), sums[1] + fold(s * h), sums[2] + fold(h * h)), h, v
-
-    def again_xy(z, h, v):
-        rows = two_rows(z)
-        high, low = split(h)
-        wide = dot(jnp.concatenate([high, low], axis=1), kx_ref[...])
+    first_xy(0, quarter)
+    first_xy(quarter, quarter)
+    pick_part(2)
+    first_xy(2 * quarter, quarter)
+    pass_up(0)
+    pick_part(3)
+    first_xy(3 * quarter, quarter)
+    for j in range(4, PARTS):
+        sums = lower_part(j - 4, sums)
+        pass_up(j - 3)
+        pick_part(j)
+    for j in range(PARTS - 4, PARTS):
+        sums = lower_part(j, sums)
+        if j == PARTS - 3:
+            pass_up(PARTS - 3)
+        if j == PARTS - 1:
+            pass_up(PARTS - 2)
+    pass_up(PARTS - 1)
+    for j in range(PARTS):
+        sums = upper_part(core, j, sums)
+    for j in range(PARTS):
+        rises[j].wait_recv()
+        sums = upper_part(1 - core, j, sums)
+
+    def again_z(i, carry):
+        cross, square = carry
+        at = [pl.ds(2 * i + e, depth, stride=pitch) for e in range(2)]
+        lines_z = [applied[own, :] for own in at]
         parts = []
+        for h in lines_z:
+            high, low = split(h)
+            parts.append(jnp.concatenate([high, high, low], axis=0))
+        result = dot(kz_ref[z_double], jnp.concatenate(parts, axis=1))
         for e in range(2):
-            own = slice(e * width, (e + 1) * width)
-            parts.append(jnp.concatenate([high[own], high[own], low[own]], axis=0))
-        tall = dot(ky_ref[y_double], jnp.concatenate(parts, axis=1))
-        total = v * h + (wide[:, :length] + wide[:, length:])
-        twice[rows, :] = total + jnp.concatenate([tall[:, :length], tall[:, length:]], axis=0)
-
-    def both(z, sums):
-        sums, h, v = full_rows(z, sums)
-        again_xy(z, h, v)
-        return sums
-
-    def z_parts(y, level):
-        parts = []
-        for e in range(2):
-            high, low = split(applied[pl.ds(level * slab * width + y + e, slab, stride=width), :])
-            parts.append(jnp.concatenate([high, high, low], axis=0))
-        return jnp.concatenate(parts, axis=1)
-
-    zero = jnp.zeros((8, length), jnp.float32)
-    sums = (zero, zero, zero)
-    while passed < PARTS:
-        pass_up(passed)
-        passed += 1
-    sums = lax.fori_loop(0, slab // 2, lambda i, c: both(2 * i, c), sums, unroll=4)
-    op = kz_ref[z_double]
-
-    def low_z(i, carry):
-        y = 2 * i
-        result = dot(op[:, : 3 * slab], z_parts(y, 0))
-        for e in range(2):
-            lifted[pl.ds(y + e, depth, stride=width), :] = result[:, e * length : (e + 1) * length]
-        return carry
-
-    lax.fori_loop(0, width // 2, low_z, 0, unroll=4)
-    for j in range(PARTS):
-        for i in range(lines // 2):
-            sums = both(slab + share * core + lines * j + 2 * i, sums)
-    for j in range(PARTS):
-        rises[j].wait_recv()
-        for i in range(lines // 2):
-            sums = both(slab + share * (1 - core) + lines * j + 2 * i, sums)
-
-    def high_z(i, carry):
-        cross, square = carry
-        y = 2 * i
-        result = dot(op[:, 3 * slab :], z_parts(y, 1))
-        for e in range(2):
-            at = pl.ds(y + e, depth, stride=width)
-            total = twice[at, :] + lifted[at, :] + result[:, e * length : (e + 1) * length]
-            twice[at, :] = total
-            cross = cross + fold(applied[at, :] * total)
+            total = twice[at[e], :] + result[:, e * length : (e + 1) * length]
+            twice[at[e], :] = total
+            cross = cross + fold(lines_z[e] * total)
             square = square + fold(total * total)
         return cross, square
 
-    cross, square = lax.fori_loop(0, width // 2, high_z, (zero, zero), unroll=4)
+    cross, square = lax.fori_loop(0, width // 2, again_z, (zero, zero), unroll=4)
 
     def whole(block):
         return jnp.sum(block, axis=(0, 1), keepdims=True)
@@ -345,8 +341,7 @@
     by_s, by_h, by_b = a2 * a, tau * (a2 + a), tau * tau
 
     def density(z):
-        rows = pl.ds(pl.multiple_of(z * width, width), lines * width)
-        u = by_s * state[rows, :] - by_h * applied[rows, :] + by_b * twice[rows, :]
+        u = by_s * lines_of(state, z, lines) - by_h * lines_of(applied, z, lines) + by_b * lines_of(twice, z, lines)
         return (factor * (u * u)).reshape(lines, 2, piece, length)
 
     halves = {}
@@ -429,8 +424,9 @@
     dma = pltpu.SemaphoreType.DMA
     part = (PARTS, lines, 2, piece, length)
     flat = (depth * width, length)
+    padded = (depth * (width + PAD), length)
     column_part = (lines, piece, length)
-    constants = (x_operator(length), line_operators(depth, True), line_operators(width, False))
+    constants = (x_operator(length), line_operators(depth), line_operators(width))
     anywhere = pl.BlockSpec(memory_space=pltpu.HBM)
     return pl.pallas_call(
         functools.partial(kernel, n_frag, n_band, depth, width, length),
@@ -440,10 +436,9 @@
         scratch_shapes=[
             pltpu.VMEM(flat, jnp.bfloat16),
             *[pltpu.VMEM(constant.shape, jnp.bfloat16) for constant in constants],
-            pltpu.VMEM(flat, f32),
-            pltpu.VMEM(flat, f32),
-            pltpu.VMEM(flat, f32),
-            pltpu.VMEM(flat, f32),
+            pltpu.VMEM(padded, f32),
+            pltpu.VMEM(padded, f32),
+            pltpu.VMEM(padded, f32),
             pltpu.VMEM((depth, 2, piece, length), f32),
             pltpu.VMEM((n_band, slab, piece, length), f32),
             pltpu.VMEM(part, f32),

time: 63.4 us -> 53.3 us (0.84)
  Pallas kernels: 56.8 us -> 50.6 us
  local copies, waits for them, and re-layouts: 5.7 us -> 1.87 us
    pallas_call x1, Pallas kernels: 56.8 us -> 50.6 us  [body(): pl.pallas_call(functools.partial(kernel, n_frag, n_band, depth, width, le...]
    unnamed x11 -> x1, local copies, waits for them, and re-layouts: 5.7 us -> 1.87 us
where the time goes in v3:
time: 53.3 us; the launch traced here: 53.1 us
  Pallas kernels  50.6 us (95%)
  local copies, waits for them, and re-layouts  1.87 us (4%)
  between operations  0.66 us (1%)
    pallas_call x1, Pallas kernels, body(): pl.pallas_call(functools.partial(kernel, n_frag, n_band, depth, width, le...  50.6 us
    unnamed x1, local copies, waits for them, and re-layouts  1.87 us

profile of v3, /device:TPU:0, one launch (start us, length us, event | category | flops | bytes accessed | tf_op | source)
XLA Modules:
  0.0 53.1 jit_solution(4886953484725689872)
XLA Ops:
  0.7 50.6 %fragment_step.1 = f32[32,32,128]{2,1,0:T(8,128)} custom-call(s32[1,1]{1,0:T(1,128)S(6)} %copy.8.code_ref, bf16[4096,128]{1,0:T(8,128)(2,1)} %bitcast.1, f32[32,32,128]{2,1,0:T(8,128)} %pot_ref.1, bf16[256,256]{1,0:T(8,128)(2,1)} %constant.4.clone.kx_hbm, bf16[2,64,192]{2,1,0:T(8,128)(2,1)} %constant.5.clone.kz_hbm.ky_hbm, ...), custom_call_target="tpu_custom_call" | custom-call | tf_op jit(solution)/shard_map/fragment_step/pallas_call | solution.py:431
  51.2 1.9 %copy.9 = f32[32,32,128]{2,1,0:T(8,128)} copy(f32[32,32,128]{2,1,0:T(8,128)} %fragment_step.1) | data formatting | bytes 1048576
